TPU v7x, 32 devices: a whole 2x2x4 slice. The times are simulated.
32 devices in a mesh: section: 4 (over x, core), fsdp: 8 (over z, y).
Axes of the slice: x: 2, y: 2, z: 4, core: 2. Of those that a mesh axis runs over, the one named last changes fastest.
Arguments:
- produced: bfloat16 [4, 24, 256, 4096], P('section', 'fsdp'), may hold values from -6 to 6
- lengths: int32 [4, 24], P('section', 'fsdp'), may hold values from 64 to 256, as said below
- active: int32 [4, 24, 4], P('section', 'fsdp'), may hold values from 0 to 7, all different within a row
- window_blocks: int32 [8], replicated, may hold values from 0 to 249, as said below
- triplets: int32 [4, 8, 3], P('section'), may hold values from 0 to 23, as said below
- teacher: float32 [4, 8], P('section'), may hold values from -60 to 60
- norm_gain: bfloat16 [4096], P('fsdp'), may hold values from 0.5 to 1.5
- head: bfloat16 [32000, 4096], P(None, 'fsdp'), may hold values from -0.09375 to 0.09375
Outputs:
- losses: float32 [4], P('section')
- produced_grad: bfloat16 [4, 24, 256, 4096], P('section', 'fsdp')
- head_grad: float32 [1024, 4096], P(None, 'fsdp')
- gain_grad: float32 [4096], P('fsdp')
Inputs may be any that keep to these rules, and one draw needn't show every extreme that they name: `lengths`: every device's first sequence holds 256 tokens, and some sequence holds 64. `active`: each row names 4 different slots. `window_blocks`: ids are distinct. `triplets`: each sequence of a group stands in exactly one triplet, once.
All inputs are finite; a program needn't handle non-finite values.
Results may differ from a plain program's by a relative error of at most 0.0051.
Values may be sent and summed in bfloat16 or wider, within the bound.
A program may use at most 192 MiB of HBM per device.

v0:
```python
import jax
import jax.numpy as jnp
from jax import lax
from jax.sharding import PartitionSpec as P

D = 4096
BLOCK = 128
U = 8
LEN = 256
SEQ_DEV = 3
eps = 1e-05
loss_scale = 256.0


def passed_along(block, axis, distance):
    devices = range(lax.axis_size(axis))
    route = [((i - distance) % len(devices), i) for i in devices]
    return lax.ppermute(block, axis, route)


def pool_terms(logits):
    smooth = jax.nn.softplus(logits)
    return (jnp.log1p(smooth), jax.nn.sigmoid(logits) / (1.0 + smooth))


def local(produced, lengths, active, window_blocks, triplets, teacher, norm_gain, head):
    sections, shards = (lax.axis_size("section"), lax.axis_size("fsdp"))
    group_data = jnp.concatenate([triplets[0].astype(jnp.float32), teacher[0][:, None]], axis=1)
    group_data = passed_along(group_data, "section", -1)
    triplet_rows = group_data[:, :3].astype(jnp.int32)
    target = group_data[:, 3]
    columns = head.shape[1]
    own_blocks = U // sections
    block_ids = lax.dynamic_slice(
        window_blocks, (lax.axis_index("section") * own_blocks,), (own_blocks,)
    )
    local_rows = head.reshape(head.shape[0] // BLOCK, BLOCK, columns)[block_ids].reshape(
        own_blocks * BLOCK, columns
    )
    piece = lax.all_gather(local_rows, "fsdp", axis=1, tiled=True)
    window = lax.all_gather(piece, "section", axis=0, tiled=True)
    gain_full = lax.all_gather(norm_gain, "fsdp", axis=0, tiled=True)
    gain32 = gain_full.astype(jnp.float32)
    tokens = produced.reshape(SEQ_DEV * LEN, D)
    widened = tokens.astype(jnp.float32)
    inv_rms = lax.rsqrt(jnp.mean(widened * widened, axis=1, keepdims=True) + eps)
    normed = (widened * inv_rms * gain32).astype(jnp.bfloat16)
    seq_len_row = lengths[0]
    slot_table = active[0]
    position = jnp.arange(LEN, dtype=jnp.int32)
    weight = (position[None, :] < seq_len_row[:, None]).astype(jnp.float32) / seq_len_row[
        :, None
    ].astype(jnp.float32)
    slot_range = jnp.arange(U, dtype=jnp.int32)
    onehot = (slot_table[:, :, None] == slot_range[None, None, :]).astype(jnp.float32)
    chosen = jnp.sum(onehot, axis=1)
    spread = jnp.repeat(chosen, BLOCK, axis=1)
    logits = jnp.einsum("td,jd->tj", normed, window, preferred_element_type=jnp.float32)
    values, slopes = pool_terms(logits.reshape(SEQ_DEV, LEN, U * BLOCK))
    pooled = jnp.sum(weight[:, :, None] * values, axis=1) * spread
    all_pooled = lax.all_gather(pooled, "fsdp", axis=0, tiled=True)
    query_rows = all_pooled[triplet_rows[:, 0]]
    positive = all_pooled[triplet_rows[:, 1]]
    negative = all_pooled[triplet_rows[:, 2]]
    margin = jnp.sum(query_rows * (positive - negative), axis=1)
    deviation = margin - target
    loss_value = passed_along(jnp.mean(deviation * deviation).reshape(1), "section", 1)
    grad_margin = loss_scale * 2.0 * deviation / triplets.shape[1]
    first_row = lax.axis_index("fsdp") * SEQ_DEV
    own_rows = first_row + jnp.arange(SEQ_DEV, dtype=jnp.int32)
    query_hits = (triplet_rows[:, 0][:, None] == own_rows[None, :]).astype(jnp.float32)
    positive_hits = (triplet_rows[:, 1][:, None] == own_rows[None, :]).astype(jnp.float32)
    negative_hits = (triplet_rows[:, 2][:, None] == own_rows[None, :]).astype(jnp.float32)
    query_term = grad_margin[:, None] * (positive - negative)
    other_term = grad_margin[:, None] * query_rows
    grad_pooled = jnp.einsum("ts,tj->sj", query_hits, query_term, precision=lax.Precision.HIGHEST)
    grad_pooled = grad_pooled + jnp.einsum(
        "ts,tj->sj", positive_hits - negative_hits, other_term, precision=lax.Precision.HIGHEST
    )
    grad_values = grad_pooled * spread
    grad_logits = (weight[:, :, None] * grad_values[:, None, :] * slopes).astype(jnp.bfloat16)
    grad_logits = grad_logits.reshape(SEQ_DEV * LEN, U * BLOCK)
    head_part = jnp.einsum(
        "tj,td->jd", grad_logits, normed, preferred_element_type=jnp.float32
    ).astype(jnp.bfloat16)
    rows = U * BLOCK // sections
    parts = lax.all_to_all(
        head_part.reshape(sections, rows, D), "section", split_axis=0, concat_axis=0
    )
    mine = jnp.sum(parts.astype(jnp.float32), axis=0).astype(jnp.bfloat16)
    parts = lax.all_to_all(mine.reshape(rows, shards, columns), "fsdp", split_axis=1, concat_axis=0)
    parts = parts.reshape(shards, rows, columns)
    mine = jnp.sum(parts.astype(jnp.float32), axis=0).astype(jnp.bfloat16)
    head_piece = lax.all_gather(mine, "section", axis=0, tiled=True).astype(jnp.float32)
    grad_normed = jnp.dot(grad_logits, window, preferred_element_type=jnp.float32)
    gain_part = jnp.sum(grad_normed * widened * inv_rms, axis=0)
    scaled = grad_normed * gain32
    grad_tokens = inv_rms * scaled - widened * (inv_rms * inv_rms * inv_rms) * jnp.mean(
        scaled * widened, axis=1, keepdims=True
    )
    outgoing = grad_tokens.astype(jnp.bfloat16).reshape(1, SEQ_DEV, LEN, D)
    gain_piece = lax.psum_scatter(gain_part, "fsdp", scatter_dimension=0, tiled=True)
    gain_piece = lax.psum(gain_piece, "section")
    return (loss_value, outgoing, head_piece, gain_piece)


def solution(mesh):
    return jax.shard_map(
        local,
        mesh=mesh,
        in_specs=(
            P("section", "fsdp", None, None),
            P("section", "fsdp"),
            P("section", "fsdp", None),
            P(),
            P("section", None, None),
            P("section", None),
            P("fsdp"),
            P(None, "fsdp"),
        ),
        out_specs=(P("section"), P("section", "fsdp", None, None), P(None, "fsdp"), P("fsdp")),
        check_vma=False,
    )
```

profile of v0, /device:TPU:0, one launch (start us, length us, event | category | flops | bytes accessed | tf_op | source)
XLA Modules:
  0.0 411.1 jit_solution(8364398150087656315)
XLA Ops:
  7.2 0.0 all-gather.6.cloned.1.call-start
  7.2 0.7 compare_select_fusion.3
  8.0 2.2 gather_fusion
  10.2 0.0 all-gather.6.cloned.1.call-update
  10.2 0.0 all-gather.8.cloned.1.call-start
  10.3 53.4 %all-gather.6.cloned.1.call-done = bf16[256,4096]{1,0:T(8,128)(2,1)} async-done(((bf16[256,512]{1,0:T(8,128)(2,1)}), bf16[256,4096]{1,0:T(8,128)(2,1)}) %all-gather.6.cloned.1.call-update) | async-done | bytes 2097168 | tf_op jit(solution)/shard_map/all_gather | solution.py:40
  63.7 0.0 all-gather.8.cloned.1.call-update
  63.7 0.7 convert_element_type.86
  64.4 0.7 pad_maximum_fusion
  65.1 0.2 collective-permute-start
  65.3 0.7 copy.27
  65.9 0.7 reshape.187
  66.6 26.1 %all-gather = bf16[8,1,512]{2,1,0:T(2,128)(2,1)S(1)} all-gather(bf16[1,1,512]{2,1,0:T(2,128)(2,1)S(1)} %reshape.187), channel_id=1, replica_groups=mesh['section'=4,'fsdp'=8] {'fsdp'}, dimensions={0}, use_global_device_ids=true | all-gather | bytes 9216 | tf_op jit(solution)/shard_map/all_gather | solution.py:42
  92.8 0.0 copy-start
  92.8 0.1 convert_reduce_fusion
  92.9 0.8 bitcast_convert_fusion
  93.7 0.9 convert_divide_fusion
  94.6 4.1 %fusion.3 = f32[3,256]{1,0:T(4,128)S(1)} fusion(bf16[1,3,256,4096]{3,2,1,0:T(8,128)(2,1)} %param.8), kind=kLoop, calls=%fused_computation.13 | loop fusion | flops 9436416 | bytes 6294528 | tf_op jit(solution)/shard_map/reduce_sum | solution.py:46
  98.7 0.1 broadcast_bitcast_fusion
  98.8 0.0 copy-done
  98.8 5.4 %fusion.5 = bf16[1,3,256,4096]{3,2,1,0:T(8,128)(2,1)} fusion(bf16[1,3,256,4096]{3,2,1,0:T(8,128)(2,1)S(1)} %copy-done, f32[4096]{0:T(1024)S(1)} %bitcast.97, f32[3,256]{1,0:T(4,128)S(1)} %add_rsqrt_fusion), kind=kLoop, calls=%fused_computation.15 | loop fusion | flops 12582912 | bytes 12602368 | tf_op jit(solution)/shard_map/convert_element_type | solution.py:47
  104.2 0.0 collective-permute-done
  104.3 17.4 %all-gather.8.cloned.1.call-done = bf16[1024,4096]{1,0:T(8,128)(2,1)} async-done(((bf16[256,4096]{1,0:T(8,128)(2,1)}), bf16[1024,4096]{1,0:T(8,128)(2,1)}) %all-gather.8.cloned.1.call-update) | async-done | bytes 8388624 | tf_op jit(solution)/shard_map/all_gather | solution.py:41
  121.7 11.2 %fusion.18 = (u8[256,1024]{1,0:T(8,128)(4,1)S(1)}, f32[3,256,1024]{2,1,0:T(8,128)S(1)}) fusion(bf16[1024,4096]{1,0:T(8,128)(2,1)} %all-gather.8.cloned.1.call-done, bf16[1,3,256,4096]{3,2,1,0:T(8,128)(2,1)} %param.8, f32[4096]{0:T(1024)S(1)} %bitcast.98, f32[3,256]{1,0:T(4,128)S(1)} %add_rsqrt_fusion), kind=kOutput, calls=%fused_computation.34 | convolution fusion | flops 6458703872 | bytes 18107392 | tf_op jit(solution)/shard_map/td,jd->tj/dot_general | solution.py:58
  133.0 0.0 copy-start.2
  133.0 3.0 multiply_reduce_fusion
  136.0 0.0 copy-done.2
  136.0 30.8 %all-gather.1 = f32[8,3,1024]{2,1,0:T(4,128)S(1)} all-gather(f32[1,3,1024]{2,1,0:T(4,128)S(1)} %fusion.22), channel_id=1, replica_groups=mesh['section'=4,'fsdp'=8] {'fsdp'}, dimensions={0}, use_global_device_ids=true | all-gather | bytes 110592 | tf_op jit(solution)/shard_map/all_gather | solution.py:61
  166.7 0.1 reshape.190
  166.8 0.6 gather_fusion.1
  167.4 0.6 gather_fusion.3
  167.9 0.6 gather_fusion.2
  168.5 0.1 multiply_reduce_fusion.1
  168.6 0.3 fusion.19
  169.0 0.3 fusion.17
  169.2 3.7 multiply_convert_fusion
  172.9 0.0 copy-start.1
  172.9 10.4 %convolution_convert_fusion = bf16[1024,4096]{1,0:T(8,128)(2,1)S(1)} fusion(bf16[768,1024]{1,0:T(8,128)(2,1)S(1)} %bitcast.94, bf16[768,4096]{1,0:T(8,128)(2,1)} %bitcast.92), kind=kOutput, calls=%fused_computation.24 | convolution fusion | flops 6446645248 | bytes 16252928 | tf_op jit(solution)/shard_map/tj,td->jd/dot_general | solution.py:83
  183.3 0.0 copy-done.1
  183.3 96.9 %all_to_all.14 = bf16[4,256,4096]{2,1,0:T(8,128)(2,1)} all-to-all(bf16[4,256,4096]{2,1,0:T(8,128)(2,1)S(1)} %bitcast.90), channel_id=1, replica_groups=mesh['section'=4,'fsdp'=8] {'section'}, dimensions={0} | all-to-all | bytes 16777216 | tf_op jit(solution)/shard_map/all_to_all | solution.py:87
  280.2 6.9 %reduce_sum.96 = bf16[256,4096]{1,0:T(8,128)(2,1)} reduce(bf16[4,256,4096]{2,1,0:T(8,128)(2,1)} %all_to_all.14, bf16[]{:T(256)} %constant.44.clone.1), dimensions={0}, to_apply=%region_6.7 | reduce | flops 3145728 | bytes 10485762 | tf_op jit(solution)/shard_map/reduce_sum | solution.py:90
  287.1 0.0 copy-start.3
  287.1 3.3 copy.15
  290.4 2.4 copy.16
  292.8 5.4 %all-to-all-start.1 = ((bf16[1,256,8,512]{3,1,0,2:T(8,128)(2,1)}), bf16[1,256,8,512]{3,1,0,2:T(8,128)(2,1)S(1)}, u32[]{:S(2)}, u32[]{:S(2)}) async-start(bf16[1,256,8,512]{3,1,0,2:T(8,128)(2,1)} %copy.16), calls=%async_computation.1 | async-start | bytes 4194304 | tf_op jit(solution)/shard_map/all_to_all | solution.py:91
  298.2 0.0 all-gather.10.cloned.1.call-start
  298.3 0.0 copy-done.3
  298.3 0.6 dynamic-slice
  299.5 0.6 fusion.42
  300.8 1.2 collective-permute-start.1
  302.0 14.1 %fusion.11 = (f32[4096]{0:T(1024)S(1)}, f32[768]{0:T(1024)S(1)}, f32[768,4096]{1,0:T(8,128)}) fusion(bf16[1,3,256,4096]{3,2,1,0:T(8,128)(2,1)} %param.8, f32[768]{0:T(1024)S(1)} %rsqrt.16, f32[4096]{0:T(1024)S(1)} %bitcast.99, bf16[768,1024]{1,0:T(8,128)(2,1)} %bitcast.95, bf16[1024,4096]{1,0:T(8,128)(2,1)} %all-gather.8.cloned.1.call-done), kind=kOutput, calls=%fused_computation.21 | convolution fusion | flops 6464465920 | bytes 28874752 | tf_op jit(solution)/shard_map/dot_general | solution.py:95
  316.1 30.0 %all-to-all-done.1 = bf16[1,256,8,512]{3,1,0,2:T(8,128)(2,1)S(1)} async-done(((bf16[1,256,8,512]{3,1,0,2:T(8,128)(2,1)}), bf16[1,256,8,512]{3,1,0,2:T(8,128)(2,1)S(1)}, u32[]{:S(2)}, u32[]{:S(2)}) %all-to-all-start.1) | async-done | bytes 2097184 | tf_op jit(solution)/shard_map/all_to_all | solution.py:91
  346.1 1.0 reduce_sum.97
  347.1 0.0 all-gather.10.cloned.1.call-update
  347.2 35.2 %all-reduce = f32[4096]{0:T(1024)S(1)} all-reduce(f32[4096]{0:T(1024)S(1)} %get-tuple-element.4), channel_id=2, replica_groups=mesh['section'=4,'fsdp'=8] {'fsdp'}, use_global_device_ids=true, to_apply=%region_9.10.clone | all-reduce | flops 4096 | bytes 32768
  382.4 0.1 dynamic-slice.1
  382.5 6.2 %psum.7 = f32[512]{0:T(512)} all-reduce(f32[512]{0:T(512)S(1)} %dynamic-slice.1), channel_id=1, replica_groups=mesh['section'=4,'fsdp'=8] {'section'}, use_global_device_ids=true, to_apply=%region_10.11 | all-reduce | flops 512 | bytes 4096 | tf_op jit(solution)/shard_map/psum | solution.py:103
  388.7 11.4 %fusion.8 = bf16[768,4096]{1,0:T(8,128)(2,1)} fusion(bf16[1,3,256,4096]{3,2,1,0:T(8,128)(2,1)} %param.8, f32[768,4096]{1,0:T(8,128)} %get-tuple-element.16, f32[768]{0:T(1024)S(1)} %broadcast_multiply_fusion, f32[768]{0:T(1024)S(1)} %multiply_multiply_fusion, f32[4096]{0:T(1024)S(1)} %bitcast.100, f32[768]{0:T(1024)S(1)} %rsqrt.16), kind=kLoop, calls=%fused_computation.18 | loop fusion | flops 22020096 | bytes 25191424 | tf_op jit(solution)/shard_map/convert_element_type | solution.py:101
  400.0 0.0 collective-permute-done.1
  400.0 0.0 all-gather.10.cloned.1.call-done
  400.0 2.8 convert_element_type.98
  (14 shorter events, 0.1 us)
Async XLA Ops:
  7.2 56.5 %all-gather.6.cloned.1.call-start = ((), (), s32[]{:S(2)}) async-start(), calls=%async_computation.2 | async-start | bytes 2359296 | tf_op jit(solution)/shard_map/all_gather | solution.py:40
  10.2 111.5 %all-gather.8.cloned.1.call-start = ((), (), s32[]{:S(2)}) async-start(), calls=%async_computation.3 | async-start | bytes 10485760 | tf_op jit(solution)/shard_map/all_gather | solution.py:41
  65.1 39.2 %collective-permute-start = (f32[8,4]{0,1:T(4,128)S(1)}, f32[8,4]{0,1:T(4,128)S(1)}, u32[]{:S(2)}, u32[]{:S(2)}) collective-permute-start(f32[8,4]{0,1:T(4,128)S(1)} %pad_maximum_fusion), channel_id=1, source_target_pairs={{8,0},{16,8},{24,16},{0,24},{9,1},{17,9},{25,17},{1,25},{10,2},{18... | collective-permute-start | bytes 392 | tf_op jit(solution)/shard_map/ppermute | solution.py:18
  92.8 6.1 %copy-start = (bf16[1,3,256,4096]{3,2,1,0:T(8,128)(2,1)S(1)}, bf16[1,3,256,4096]{3,2,1,0:T(8,128)(2,1)}, u32[]{:S(2)}) copy-start(bf16[1,3,256,4096]{3,2,1,0:T(8,128)(2,1)} %param.8) | copy-start | bytes 18874372
  133.0 3.0 copy-start.2
  172.9 10.4 %copy-start.1 = (bf16[3,256,1024]{2,1,0:T(8,128)(2,1)}, bf16[3,256,1024]{2,1,0:T(8,128)(2,1)S(1)}, u32[]{:S(2)}) copy-start(bf16[3,256,1024]{2,1,0:T(8,128)(2,1)S(1)} %multiply_convert_fusion) | copy-start | bytes 4718596
  287.1 11.2 %copy-start.3 = (u32[32]{0:T(128)S(1)}, u32[32]{0:T(128)}, u32[]{:S(2)}) copy-start(u32[32]{0:T(128)} %constant.52) | copy-start | bytes 388
  292.8 53.3 %all-to-all-start.1 = ((bf16[1,256,8,512]{3,1,0,2:T(8,128)(2,1)}), bf16[1,256,8,512]{3,1,0,2:T(8,128)(2,1)S(1)}, u32[]{:S(2)}, u32[]{:S(2)}) async-start(bf16[1,256,8,512]{3,1,0,2:T(8,128)(2,1)} %copy.16), calls=%async_computation.1 | async-start | bytes 4194304 | tf_op jit(solution)/shard_map/all_to_all | solution.py:91
  298.2 101.8 %all-gather.10.cloned.1.call-start = ((), (), s32[]{:S(2)}) async-start(), calls=%async_computation.4 | async-start | bytes 1310720 | tf_op jit(solution)/shard_map/all_gather | solution.py:94
  300.8 99.2 %collective-permute-start.1 = (f32[1]{0:T(128)}, f32[1]{0:T(128)}, u32[]{:S(2)}, u32[]{:S(2)}) collective-permute-start(f32[1]{0:T(128)} %bitcast.12), channel_id=1, source_target_pairs={{24,0},{0,8},{8,16},{16,24},{25,1},{1,9},{9,17},{17,25},{26,2},{2,... | collective-permute-start | bytes 20 | tf_op jit(solution)/shard_map/ppermute | solution.py:18
Sparse Core Ops, SparseCore 0:
  10.6 53.0 all-gather.5
  65.2 56.4 all-gather.7
  347.3 15.0 all-gather.9
where the time goes:
time: 412 us; the launch traced here: 411 us
  blocking collectives  195 us (47%)
  waiting for transfers between devices  101 us (25%)
  other arithmetic  43 us (10%)
  matrix products  36.3 us (9%)
  between operations  16.9 us (4%)
  local copies, waits for them, and re-layouts  11.8 us (3%)
  starting transfers between devices  6.99 us (2%)
    all_to_all x1, blocking collectives, local(): lax.all_to_all(head_part.reshape(sections, rows, D), 'section', split_axi...  96.9 us
    all_gather x1, waiting for transfers between devices, local(): piece = lax.all_gather(local_rows, 'fsdp', axis=1, tiled=True)  53.4 us
    unnamed x1, blocking collectives  35.2 us
    all_gather x1, blocking collectives, local(): all_pooled = lax.all_gather(pooled, 'fsdp', axis=0, tiled=True)  30.8 us
    all_to_all x1, waiting for transfers between devices, local(): lax.all_to_all(mine.reshape(rows, shards, columns), 'fsdp', split_axis=1,...  30 us
    all_gather x1, blocking collectives, local(): gain_full = lax.all_gather(norm_gain, 'fsdp', axis=0, tiled=True)  26.1 us
    all_gather x1, waiting for transfers between devices, local(): window = lax.all_gather(piece, 'section', axis=0, tiled=True)  17.4 us
    dot_general x1, matrix products, local(): jnp.dot(grad_logits, window, preferred_element_type=jnp.float32)  14.1 us
  transfers between devices with their start and end apart: 6, of which 3 were waited for; matrix products, arithmetic and copies ran while one was open for 10% of the time, Pallas kernels for 0%

commit v1 on v0

--- a/solution.py
+++ b/solution.py
@@ -37,7 +37,12 @@
     local_rows = head.reshape(head.shape[0] // BLOCK, BLOCK, columns)[block_ids].reshape(
         own_blocks * BLOCK, columns
     )
-    piece = lax.all_gather(local_rows, "fsdp", axis=1, tiled=True)
+    ring = [local_rows]
+    for hop in range(7):
+        ring.append(lax.ppermute(ring[-1], "fsdp", [(dev, (dev + 1) % 8) for dev in range(8)]))
+    piece = jnp.roll(
+        jnp.concatenate(ring[::-1], axis=1), (lax.axis_index("fsdp") + 1) * ring[0].shape[1], axis=1
+    )
     window = lax.all_gather(piece, "section", axis=0, tiled=True)
     gain_full = lax.all_gather(norm_gain, "fsdp", axis=0, tiled=True)
     gain32 = gain_full.astype(jnp.float32)

time: 412 us -> 426 us (1.034)
  waiting for transfers between devices: 101 us -> 112 us
    ppermute x0 -> x7, waiting for transfers between devices: none -> 65.7 us  [local(): lax.ppermute(ring[-1], 'fsdp', [(dev, (dev + 1) % 8) for dev in range(8)])]
    all_gather x1 -> x0, waiting for transfers between devices: 53.4 us -> none  [local(): piece = lax.all_gather(local_rows, 'fsdp', axis=1, tiled=True)]
  transfers between devices with their start and end apart: 6 -> 12, of which waited for: 3 -> 9; matrix products, arithmetic and copies ran while one was open for 10% -> 10% of each run, Pallas kernels for 0% -> 0%
where the time goes in v1:
time: 426 us
  blocking collectives  195 us (46%)
  waiting for transfers between devices  112 us (26%)
  other arithmetic  42.9 us (10%)
  matrix products  36.3 us (9%)
  between operations  17.5 us (4%)
  local copies, waits for them, and re-layouts  11.7 us (3%)
  starting transfers between devices  9.87 us (2%)
    all_to_all x1, blocking collectives, local(): lax.all_to_all(head_part.reshape(sections, rows, D), 'section', split_axi...  96.9 us
    ppermute x7, waiting for transfers between devices, local(): lax.ppermute(ring[-1], 'fsdp', [(dev, (dev + 1) % 8) for dev in range(8)])  65.7 us
    unnamed x1, blocking collectives  35.2 us
    all_gather x1, blocking collectives, local(): all_pooled = lax.all_gather(pooled, 'fsdp', axis=0, tiled=True)  30.8 us
    all_to_all x1, waiting for transfers between devices, local(): lax.all_to_all(mine.reshape(rows, shards, columns), 'fsdp', split_axis=1,...  30 us
    all_gather x1, blocking collectives, local(): gain_full = lax.all_gather(norm_gain, 'fsdp', axis=0, tiled=True)  26.1 us
    all_gather x1, waiting for transfers between devices, local(): window = lax.all_gather(piece, 'section', axis=0, tiled=True)  16.4 us
    dot_general x1, matrix products, local(): jnp.dot(grad_logits, window, preferred_element_type=jnp.float32)  14.1 us
  transfers between devices with their start and end apart: 12, of which 9 were waited for; matrix products, arithmetic and copies ran while one was open for 10% of the time, Pallas kernels for 0%

profile of v1, /device:TPU:0, one launch (start us, length us, event | category | flops | bytes accessed | tf_op | source)
XLA Modules:
  0.0 425.6 jit_solution(4283907958190262033)
XLA Ops:
  7.2 0.0 all-gather.5.cloned.1.call-start
  7.2 0.7 compare_select_fusion.3
  8.0 1.5 gather_fusion
  9.5 3.0 collective-permute-start
  12.5 9.3 %collective-permute-done = bf16[256,512]{1,0:T(8,128)(2,1)S(1)} collective-permute-done((bf16[256,512]{1,0:T(8,128)(2,1)S(1)}, bf16[256,512]{1,0:T(8,128)(2,1)S(1)}, u32[]{:S(2)}, u32[]{:S(2)}) %collective-permute-start) | collective-permute-done | bytes 262176 | tf_op jit(solution)/shard_map/ppermute | solution.py:42
  21.9 0.0 collective-permute-start.1
  21.9 10.2 %collective-permute-done.1 = bf16[256,512]{1,0:T(8,128)(2,1)S(1)} collective-permute-done((bf16[256,512]{1,0:T(8,128)(2,1)S(1)}, bf16[256,512]{1,0:T(8,128)(2,1)S(1)}, u32[]{:S(2)}, u32[]{:S(2)}) %collective-permute-start.1) | collective-permute-done | bytes 262176 | tf_op jit(solution)/shard_map/ppermute | solution.py:42
  32.0 0.0 collective-permute-start.2
  32.1 9.3 %collective-permute-done.2 = bf16[256,512]{1,0:T(8,128)(2,1)S(1)} collective-permute-done((bf16[256,512]{1,0:T(8,128)(2,1)S(1)}, bf16[256,512]{1,0:T(8,128)(2,1)S(1)}, u32[]{:S(2)}, u32[]{:S(2)}) %collective-permute-start.2) | collective-permute-done | bytes 262176 | tf_op jit(solution)/shard_map/ppermute | solution.py:42
  41.4 0.0 collective-permute-start.3
  41.4 9.1 %collective-permute-done.3 = bf16[256,512]{1,0:T(8,128)(2,1)S(1)} collective-permute-done((bf16[256,512]{1,0:T(8,128)(2,1)S(1)}, bf16[256,512]{1,0:T(8,128)(2,1)S(1)}, u32[]{:S(2)}, u32[]{:S(2)}) %collective-permute-start.3) | collective-permute-done | bytes 262176 | tf_op jit(solution)/shard_map/ppermute | solution.py:42
  50.4 0.0 collective-permute-start.4
  50.4 9.1 %collective-permute-done.4 = bf16[256,512]{1,0:T(8,128)(2,1)S(1)} collective-permute-done((bf16[256,512]{1,0:T(8,128)(2,1)S(1)}, bf16[256,512]{1,0:T(8,128)(2,1)S(1)}, u32[]{:S(2)}, u32[]{:S(2)}) %collective-permute-start.4) | collective-permute-done | bytes 262176 | tf_op jit(solution)/shard_map/ppermute | solution.py:42
  59.5 0.0 collective-permute-start.5
  59.5 9.7 %collective-permute-done.5 = bf16[256,512]{1,0:T(8,128)(2,1)S(1)} collective-permute-done((bf16[256,512]{1,0:T(8,128)(2,1)S(1)}, bf16[256,512]{1,0:T(8,128)(2,1)S(1)}, u32[]{:S(2)}, u32[]{:S(2)}) %collective-permute-start.5) | collective-permute-done | bytes 262176 | tf_op jit(solution)/shard_map/ppermute | solution.py:42
  69.2 9.1 %collective-permute-done.6 = bf16[256,512]{1,0:T(8,128)(2,1)S(1)} collective-permute-done((bf16[256,512]{1,0:T(8,128)(2,1)S(1)}, bf16[256,512]{1,0:T(8,128)(2,1)S(1)}, u32[]{:S(2)}, u32[]{:S(2)}) %collective-permute-start.6) | collective-permute-done | bytes 262176 | tf_op jit(solution)/shard_map/ppermute | solution.py:42
  78.7 0.0 copy-start.3
  78.7 0.0 copy-start.5
  78.7 0.0 copy-start.2
  78.7 0.0 copy-start.4
  78.7 0.0 copy-start.6
  78.9 1.5 constant_dynamic-slice_fusion
  80.4 0.0 all-gather.5.cloned.1.call-update
  80.5 0.1 collective-permute-start.7
  80.6 26.1 %all-gather = bf16[8,1,512]{2,1,0:T(2,128)(2,1)S(1)} all-gather(bf16[1,1,512]{2,1,0:T(2,128)(2,1)S(1)} %reshape.187), channel_id=1, replica_groups=mesh['section'=4,'fsdp'=8] {'fsdp'}, dimensions={0}, use_global_device_ids=true | all-gather | bytes 9216 | tf_op jit(solution)/shard_map/all_gather | solution.py:47
  106.8 0.1 convert_reduce_fusion
  106.9 0.1 convert_divide_fusion
  106.9 4.1 fusion.3
  111.1 0.1 broadcast_bitcast_fusion
  111.2 8.3 %fusion.5 = bf16[1,3,256,4096]{3,2,1,0:T(8,128)(2,1)} fusion(bf16[1,3,256,4096]{3,2,1,0:T(8,128)(2,1)} %param.8, f32[4096]{0:T(1024)S(1)} %bitcast.99, f32[3,256]{1,0:T(4,128)S(1)} %add_rsqrt_fusion), kind=kLoop, calls=%fused_computation.15 | loop fusion | flops 12582912 | bytes 12602368 | tf_op jit(solution)/shard_map/convert_element_type | solution.py:52
  119.5 0.0 collective-permute-done.7
  119.5 16.4 %all-gather.5.cloned.1.call-done = bf16[1024,4096]{1,0:T(8,128)(2,1)} async-done(((bf16[256,4096]{1,0:T(8,128)(2,1)}), bf16[1024,4096]{1,0:T(8,128)(2,1)}) %all-gather.5.cloned.1.call-update) | async-done | bytes 8388624 | tf_op jit(solution)/shard_map/all_gather | solution.py:46
  136.0 11.2 %fusion.18 = (u8[256,1024]{1,0:T(8,128)(4,1)S(1)}, f32[3,256,1024]{2,1,0:T(8,128)S(1)}) fusion(bf16[1024,4096]{1,0:T(8,128)(2,1)} %all-gather.5.cloned.1.call-done, bf16[1,3,256,4096]{3,2,1,0:T(8,128)(2,1)} %param.8, f32[4096]{0:T(1024)S(1)} %bitcast.100, f32[3,256]{1,0:T(4,128)S(1)} %add_rsqrt_fusion), kind=kOutput, calls=%fused_computation.34 | convolution fusion | flops 6458703872 | bytes 18107392 | tf_op jit(solution)/shard_map/td,jd->tj/dot_general | solution.py:63
  147.2 0.0 copy-start.1
  147.2 3.0 multiply_reduce_fusion
  150.2 30.8 %all-gather.1 = f32[8,3,1024]{2,1,0:T(4,128)S(1)} all-gather(f32[1,3,1024]{2,1,0:T(4,128)S(1)} %fusion.22), channel_id=1, replica_groups=mesh['section'=4,'fsdp'=8] {'fsdp'}, dimensions={0}, use_global_device_ids=true | all-gather | bytes 110592 | tf_op jit(solution)/shard_map/all_gather | solution.py:66
  181.0 0.1 reshape.190
  181.0 0.6 gather_fusion.1
  181.6 0.6 gather_fusion.3
  182.2 0.6 gather_fusion.2
  182.8 0.1 multiply_reduce_fusion.1
  182.9 0.3 fusion.19
  183.2 0.3 fusion.17
  183.5 3.7 multiply_convert_fusion
  187.2 10.4 %convolution_convert_fusion = bf16[1024,4096]{1,0:T(8,128)(2,1)S(1)} fusion(bf16[768,1024]{1,0:T(8,128)(2,1)S(1)} %bitcast.97, bf16[768,4096]{1,0:T(8,128)(2,1)} %bitcast.92), kind=kOutput, calls=%fused_computation.24 | convolution fusion | flops 6446645248 | bytes 16252928 | tf_op jit(solution)/shard_map/tj,td->jd/dot_general | solution.py:88
  197.6 96.9 %all_to_all.14 = bf16[4,256,4096]{2,1,0:T(8,128)(2,1)} all-to-all(bf16[4,256,4096]{2,1,0:T(8,128)(2,1)S(1)} %bitcast.90), channel_id=1, replica_groups=mesh['section'=4,'fsdp'=8] {'section'}, dimensions={0} | all-to-all | bytes 16777216 | tf_op jit(solution)/shard_map/all_to_all | solution.py:92
  294.4 6.9 %reduce_sum.96 = bf16[256,4096]{1,0:T(8,128)(2,1)} reduce(bf16[4,256,4096]{2,1,0:T(8,128)(2,1)} %all_to_all.14, bf16[]{:T(256)} %constant.69.clone.1), dimensions={0}, to_apply=%region_6.7 | reduce | flops 3145728 | bytes 10485762 | tf_op jit(solution)/shard_map/reduce_sum | solution.py:95
  301.3 3.3 copy.15
  304.6 0.0 copy-start.7
  304.6 2.4 copy.16
  307.0 5.4 %all-to-all-start.1 = ((bf16[1,256,8,512]{3,1,0,2:T(8,128)(2,1)}), bf16[1,256,8,512]{3,1,0,2:T(8,128)(2,1)S(1)}, u32[]{:S(2)}, u32[]{:S(2)}) async-start(bf16[1,256,8,512]{3,1,0,2:T(8,128)(2,1)} %copy.16), calls=%async_computation.1 | async-start | bytes 4194304 | tf_op jit(solution)/shard_map/all_to_all | solution.py:96
  312.4 0.0 all-gather.7.cloned.1.call-start
  312.5 0.6 dynamic-slice
  313.8 0.6 fusion.42
  315.0 1.2 collective-permute-start.8
  316.3 14.1 %fusion.11 = (f32[4096]{0:T(1024)S(1)}, f32[768]{0:T(1024)S(1)}, f32[768,4096]{1,0:T(8,128)}) fusion(bf16[1,3,256,4096]{3,2,1,0:T(8,128)(2,1)} %param.8, f32[768]{0:T(1024)S(1)} %rsqrt.16, f32[4096]{0:T(1024)S(1)} %bitcast.101, bf16[768,1024]{1,0:T(8,128)(2,1)} %bitcast.98, bf16[1024,4096]{1,0:T(8,128)(2,1)} %all-gather.5.cloned.1.call-done), kind=kOutput, calls=%fused_computation.21 | convolution fusion | flops 6464465920 | bytes 28874752 | tf_op jit(solution)/shard_map/dot_general | solution.py:100
  330.4 30.0 %all-to-all-done.1 = bf16[1,256,8,512]{3,1,0,2:T(8,128)(2,1)S(1)} async-done(((bf16[1,256,8,512]{3,1,0,2:T(8,128)(2,1)}), bf16[1,256,8,512]{3,1,0,2:T(8,128)(2,1)S(1)}, u32[]{:S(2)}, u32[]{:S(2)}) %all-to-all-start.1) | async-done | bytes 2097184 | tf_op jit(solution)/shard_map/all_to_all | solution.py:96
  360.3 1.0 reduce_sum.97
  361.4 0.0 all-gather.7.cloned.1.call-update
  361.4 35.2 %all-reduce = f32[4096]{0:T(1024)S(1)} all-reduce(f32[4096]{0:T(1024)S(1)} %get-tuple-element.4), channel_id=2, replica_groups=mesh['section'=4,'fsdp'=8] {'fsdp'}, use_global_device_ids=true, to_apply=%region_9.10.clone | all-reduce | flops 4096 | bytes 32768
  396.6 0.1 dynamic-slice.1
  396.7 6.2 %psum.7 = f32[512]{0:T(512)} all-reduce(f32[512]{0:T(512)S(1)} %dynamic-slice.1), channel_id=1, replica_groups=mesh['section'=4,'fsdp'=8] {'section'}, use_global_device_ids=true, to_apply=%region_10.11 | all-reduce | flops 512 | bytes 4096 | tf_op jit(solution)/shard_map/psum | solution.py:108
  402.9 11.4 %fusion.8 = bf16[768,4096]{1,0:T(8,128)(2,1)} fusion(bf16[1,3,256,4096]{3,2,1,0:T(8,128)(2,1)} %param.8, f32[768,4096]{1,0:T(8,128)} %get-tuple-element.16, f32[768]{0:T(1024)S(1)} %broadcast_multiply_fusion, f32[768]{0:T(1024)S(1)} %multiply_multiply_fusion, f32[4096]{0:T(1024)S(1)} %bitcast.102, f32[768]{0:T(1024)S(1)} %rsqrt.16), kind=kLoop, calls=%fused_computation.18 | loop fusion | flops 22020096 | bytes 25191424 | tf_op jit(solution)/shard_map/convert_element_type | solution.py:106
  414.2 2.8 convert_element_type.98
  (47 shorter events, 0.6 us)
Async XLA Ops:
  7.2 128.8 %all-gather.5.cloned.1.call-start = ((), (), s32[]{:S(2)}) async-start(), calls=%async_computation.2 | async-start | bytes 10485760 | tf_op jit(solution)/shard_map/all_gather | solution.py:46
  9.5 12.4 %collective-permute-start = (bf16[256,512]{1,0:T(8,128)(2,1)S(1)}, bf16[256,512]{1,0:T(8,128)(2,1)S(1)}, u32[]{:S(2)}, u32[]{:S(2)}) collective-permute-start(bf16[256,512]{1,0:T(8,128)(2,1)S(1)} %bitcast.94), channel_id=1, source_target_pairs={{0,1},{1,2},{2,3},{3,4},{4,5},{5,6},{6,7},{7,0},{8,9},{9,10},{10,1... | collective-permute-start | bytes 786440 | tf_op jit(solution)/shard_map/ppermute | solution.py:42
  21.9 10.2 %collective-permute-start.1 = (bf16[256,512]{1,0:T(8,128)(2,1)S(1)}, bf16[256,512]{1,0:T(8,128)(2,1)S(1)}, u32[]{:S(2)}, u32[]{:S(2)}) collective-permute-start(bf16[256,512]{1,0:T(8,128)(2,1)S(1)} %collective-permute-done), channel_id=1, source_target_pairs={{0,1},{1,2},{2,3},{3,4},{4,5},{5,6},{6,7},{7,0},{8,9},{9,10},{10,1... | collective-permute-start | bytes 786440 | tf_op jit(solution)/shard_map/ppermute | solution.py:42
  32.0 9.3 %collective-permute-start.2 = (bf16[256,512]{1,0:T(8,128)(2,1)S(1)}, bf16[256,512]{1,0:T(8,128)(2,1)S(1)}, u32[]{:S(2)}, u32[]{:S(2)}) collective-permute-start(bf16[256,512]{1,0:T(8,128)(2,1)S(1)} %collective-permute-done.1), channel_id=1, source_target_pairs={{0,1},{1,2},{2,3},{3,4},{4,5},{5,6},{6,7},{7,0},{8,9},{9,10},{10,1... | collective-permute-start | bytes 786440 | tf_op jit(solution)/shard_map/ppermute | solution.py:42
  41.4 9.1 %collective-permute-start.3 = (bf16[256,512]{1,0:T(8,128)(2,1)S(1)}, bf16[256,512]{1,0:T(8,128)(2,1)S(1)}, u32[]{:S(2)}, u32[]{:S(2)}) collective-permute-start(bf16[256,512]{1,0:T(8,128)(2,1)S(1)} %collective-permute-done.2), channel_id=1, source_target_pairs={{0,1},{1,2},{2,3},{3,4},{4,5},{5,6},{6,7},{7,0},{8,9},{9,10},{10,1... | collective-permute-start | bytes 786440 | tf_op jit(solution)/shard_map/ppermute | solution.py:42
  50.4 9.1 %collective-permute-start.4 = (bf16[256,512]{1,0:T(8,128)(2,1)S(1)}, bf16[256,512]{1,0:T(8,128)(2,1)S(1)}, u32[]{:S(2)}, u32[]{:S(2)}) collective-permute-start(bf16[256,512]{1,0:T(8,128)(2,1)S(1)} %collective-permute-done.3), channel_id=1, source_target_pairs={{0,1},{1,2},{2,3},{3,4},{4,5},{5,6},{6,7},{7,0},{8,9},{9,10},{10,1... | collective-permute-start | bytes 786440 | tf_op jit(solution)/shard_map/ppermute | solution.py:42
  59.5 9.7 %collective-permute-start.5 = (bf16[256,512]{1,0:T(8,128)(2,1)S(1)}, bf16[256,512]{1,0:T(8,128)(2,1)S(1)}, u32[]{:S(2)}, u32[]{:S(2)}) collective-permute-start(bf16[256,512]{1,0:T(8,128)(2,1)S(1)} %collective-permute-done.4), channel_id=1, source_target_pairs={{0,1},{1,2},{2,3},{3,4},{4,5},{5,6},{6,7},{7,0},{8,9},{9,10},{10,1... | collective-permute-start | bytes 786440 | tf_op jit(solution)/shard_map/ppermute | solution.py:42
  69.2 9.1 %collective-permute-start.6 = (bf16[256,512]{1,0:T(8,128)(2,1)S(1)}, bf16[256,512]{1,0:T(8,128)(2,1)S(1)}, u32[]{:S(2)}, u32[]{:S(2)}) collective-permute-start(bf16[256,512]{1,0:T(8,128)(2,1)S(1)} %collective-permute-done.5), channel_id=1, source_target_pairs={{0,1},{1,2},{2,3},{3,4},{4,5},{5,6},{6,7},{7,0},{8,9},{9,10},{10,1... | collective-permute-start | bytes 786440 | tf_op jit(solution)/shard_map/ppermute | solution.py:42
  78.7 1.8 copy-start.3
  78.7 1.8 copy-start.5
  78.7 1.9 copy-start.2
  78.7 1.9 copy-start.4
  78.7 28.1 %copy-start.6 = (s32[1,3]{1,0:T(1,128)S(1)}, s32[1,3]{1,0:T(1,128)}, u32[]{:S(2)}) copy-start(s32[1,3]{1,0:T(1,128)} %param.9) | copy-start | bytes 40
  80.5 39.0 %collective-permute-start.7 = (f32[8,4]{0,1:T(4,128)S(1)}, f32[8,4]{0,1:T(4,128)S(1)}, u32[]{:S(2)}, u32[]{:S(2)}) collective-permute-start(f32[8,4]{0,1:T(4,128)S(1)} %pad_maximum_fusion), channel_id=1, source_target_pairs={{8,0},{16,8},{24,16},{0,24},{9,1},{17,9},{25,17},{1,25},{10,2},{18... | collective-permute-start | bytes 392 | tf_op jit(solution)/shard_map/ppermute | solution.py:18
  147.2 3.0 copy-start.1
  187.1 10.4 %copy-start = (bf16[3,256,1024]{2,1,0:T(8,128)(2,1)}, bf16[3,256,1024]{2,1,0:T(8,128)(2,1)S(1)}, u32[]{:S(2)}) copy-start(bf16[3,256,1024]{2,1,0:T(8,128)(2,1)S(1)} %multiply_convert_fusion) | copy-start | bytes 4718596
  304.6 7.9 %copy-start.7 = (u32[32]{0:T(128)S(1)}, u32[32]{0:T(128)}, u32[]{:S(2)}) copy-start(u32[32]{0:T(128)} %constant.77) | copy-start | bytes 388
  307.0 53.3 %all-to-all-start.1 = ((bf16[1,256,8,512]{3,1,0,2:T(8,128)(2,1)}), bf16[1,256,8,512]{3,1,0,2:T(8,128)(2,1)S(1)}, u32[]{:S(2)}, u32[]{:S(2)}) async-start(bf16[1,256,8,512]{3,1,0,2:T(8,128)(2,1)} %copy.16), calls=%async_computation.1 | async-start | bytes 4194304 | tf_op jit(solution)/shard_map/all_to_all | solution.py:96
  312.4 101.8 %all-gather.7.cloned.1.call-start = ((), (), s32[]{:S(2)}) async-start(), calls=%async_computation.3 | async-start | bytes 1310720 | tf_op jit(solution)/shard_map/all_gather | solution.py:99
  315.0 99.2 %collective-permute-start.8 = (f32[1]{0:T(128)}, f32[1]{0:T(128)}, u32[]{:S(2)}, u32[]{:S(2)}) collective-permute-start(f32[1]{0:T(128)} %bitcast.12), channel_id=1, source_target_pairs={{24,0},{0,8},{8,16},{16,24},{25,1},{1,9},{9,17},{17,25},{26,2},{2,... | collective-permute-start | bytes 20 | tf_op jit(solution)/shard_map/ppermute | solution.py:18
Sparse Core Ops, SparseCore 0:
  80.6 55.3 all-gather.4
  361.5 15.0 all-gather.6
